TPU v7x, 512 devices: a whole 4x8x8 slice. The times are simulated.
512 devices in a mesh: aux: 8 (over z), ao: 16 (over y, core), orb: 4 (over x).
Axes of the slice: x: 4, y: 8, z: 8, core: 2. Of those that a mesh axis runs over, the one named last changes fastest.
Arguments:
- integrals: bfloat16 [128, 16, 4, 128, 128], P('aux', 'ao', None, 'orb'), may hold values from -6 to 6
- partner: int32 [16, 4], P('ao'), may hold values from 0 to 15
- pair_count: int32 [16], P('ao'), may hold values from 1 to 4
- occupied_coeff: bfloat16 [2048, 512], P('ao', 'orb'), may hold values from -0.25 to 0.25
- occupied_domain: int32 [16, 4], P('ao', 'orb'), may hold values 0 or 1
- virtual_coeff: bfloat16 [2048, 8192], P('aux', 'ao'), may hold values from -0.125 to 0.125
- virtual_domain: int32 [16, 64], P(None, 'ao'), may hold values 0 or 1
Outputs:
- transformed: bfloat16 [128, 512, 8192], P('aux', 'orb', 'ao')
All inputs are finite; a program needn't handle non-finite values. No bound on the sum of `occupied_domain` or of `virtual_domain` on one device may be relied on, other than what follows from the above.
Results may differ from a plain program's by a relative error of at most 0.0049.
Values may be sent and summed in bfloat16 or wider, within the bound.
A program may use at most 64 MiB of HBM per device.

v0:
```python
import jax
import jax.numpy as jnp
from jax import lax
from jax.sharding import PartitionSpec as P


def local(
    integrals, partner, pair_count, occupied_coeff, occupied_domain, virtual_coeff, virtual_domain
):
    block_size = integrals.shape[4]
    slab_rows = integrals.shape[0]
    local_blocks = integrals.shape[1]
    slot_count = integrals.shape[2]
    occ_width = occupied_coeff.shape[1]
    domain_wire = occupied_domain.astype(jnp.bfloat16)
    all_occ, all_domain = (
        lax.all_gather(occupied_coeff, "ao", axis=0, tiled=True),
        lax.all_gather(domain_wire, "ao", axis=0, tiled=True),
    )
    occ_mask = jnp.repeat(jnp.repeat(all_domain, block_size, axis=0), block_size, axis=1)
    occ_masked = all_occ * occ_mask
    block_total = all_domain.shape[0]
    picked = occ_masked.reshape(block_total, block_size, occ_width)[partner]
    slots = jnp.arange(slot_count, dtype=jnp.int32)
    live = (slots[None, :] < pair_count[:, None]).astype(jnp.bfloat16)
    picked = picked * live[:, :, None, None]
    all_columns = lax.all_to_all(picked, "orb", split_axis=2, concat_axis=3, tiled=True)
    partial_term = jnp.einsum(
        "nkri,pnkrv->pinv", all_columns, integrals, preferred_element_type=jnp.float32
    )
    half_wide = lax.psum_scatter(partial_term, "orb", scatter_dimension=1, tiled=True)
    half_local = half_wide.reshape(slab_rows, occ_width, local_blocks * block_size).astype(
        jnp.bfloat16
    )
    vir_rows = lax.all_gather(virtual_coeff, "aux", axis=0, tiled=True)
    vir_mask = jnp.repeat(
        jnp.repeat(virtual_domain, block_size, axis=0), block_size, axis=1
    ).astype(jnp.bfloat16)
    vir_masked = vir_rows * vir_mask
    vir_width = vir_masked.shape[1]
    piece = lax.all_gather(half_local, "ao", axis=2, tiled=True)
    count = piece.shape[2]
    flat = piece.reshape(slab_rows * occ_width, count)
    product = jnp.dot(flat, vir_masked, preferred_element_type=jnp.float32)
    result = product.reshape(slab_rows, occ_width, vir_width)
    return result.astype(jnp.bfloat16)


def solution(mesh):
    placed = (
        P("aux", "ao", None, "orb", None),
        P("ao", None),
        P("ao"),
        P("ao", "orb"),
        P("ao", "orb"),
        P("aux", "ao"),
        P(None, "ao"),
    )
    return jax.shard_map(
        local, mesh=mesh, in_specs=placed, out_specs=P("aux", "orb", "ao"), check_vma=False
    )
```

profile of v0, /device:TPU:1, one launch (start us, length us, event | category | flops | bytes accessed | tf_op | source)
XLA Modules:
  0.0 215.5 jit_solution(4892264346600140509)
XLA Ops:
  8.7 0.7 fusion.11
  9.4 1.3 dynamic-slice
  10.7 0.7 dynamic-update-slice
  11.3 29.8 %all-reduce = bf16[16]{0:T(256)(128)(2,1)S(1)} all-reduce(bf16[16]{0:T(256)(128)(2,1)S(1)} %dynamic-update-slice), channel_id=1, replica_groups=mesh['aux'=8,'ao'=16,'orb'=4] {'ao'}, use_global_device_ids=true, to_apply=%add | all-reduce | flops 16 | bytes 64
  41.1 0.1 broadcast_bitcast_fusion
  41.2 16.4 %all_gather.14 = bf16[2048,128]{1,0:T(8,128)(2,1)S(1)} all-gather(bf16[128,128]{1,0:T(8,128)(2,1)} %param.10), channel_id=1, replica_groups=mesh['aux'=8,'ao'=16,'orb'=4] {'ao'}, dimensions={0}, use_global_device_ids=true | all-gather | bytes 557056 | tf_op jit(solution)/shard_map/all_gather | solution.py:17
  57.6 0.3 broadcast_multiply_fusion
  58.0 0.6 gather_fusion
  58.5 0.1 bitcast_multiply_fusion.1
  58.6 0.1 copy.14
  58.7 7.3 %all_to_all.15 = bf16[1,4,128,128]{3,1,0,2:T(4,128)(2,1)S(1)} all-to-all(bf16[1,4,128,128]{3,1,0,2:T(4,128)(2,1)S(1)} %copy.14), channel_id=1, replica_groups=mesh['aux'=8,'ao'=16,'orb'=4] {'orb'}, dimensions={2} | all-to-all | bytes 262144 | tf_op jit(solution)/shard_map/all_to_all | solution.py:27
  66.1 0.1 copy.16
  66.1 0.1 reshape.70
  66.2 2.7 %convolution_bitcast_fusion = f32[16,512,1,128]{3,1,0,2:T(8,128)} fusion(bf16[4,32,512,1]{2,1,0,3:T(8,128)(2,1)S(1)} %reshape.70, bf16[16,1,4,32,128]{4,3,2,1,0:T(8,128)(2,1)S(1)} %copy-done), kind=kOutput, calls=%fused_computation.3 | convolution fusion | flops 268435456 | bytes 4849664 | tf_op jit(solution)/shard_map/nkri,pnkrv->pinv/dot_general | solution.py:28
  68.9 0.0 all-gather.4.cloned.1.call-start
  69.0 0.5 all-gather.4.cloned.1.call-update
  69.5 0.0 all-gather.6.cloned.1.call-start
  69.6 51.7 %reduce-scatter.2.cloned.1.call-done = f32[16,128,1,128]{3,1,0,2:T(8,128)} async-done(((f32[16,512,1,128]{3,1,0,2:T(8,128)}), f32[16,128,1,128]{3,1,0,2:T(8,128)}) %reduce-scatter.2.cloned.1.call-update) | async-done | bytes 1048592 | tf_op jit(solution)/shard_map/reduce_scatter | solution.py:31
  121.2 2.1 convert_element_type.34
  123.4 0.1 copy.17
  123.5 69.4 %all-gather.6.cloned.1.call-done = bf16[16,128,1,2048]{3,1,0,2:T(8,128)(2,1)} async-done(((bf16[16,128,1,128]{3,1,0,2:T(8,128)(2,1)}), bf16[16,128,1,2048]{3,1,0,2:T(8,128)(2,1)}) %all-gather.6.cloned.1.call-update) | async-done | bytes 8388624 | tf_op jit(solution)/shard_map/all_gather | solution.py:41
  192.9 0.1 broadcast_in_dim.21
  193.0 5.8 %broadcast_in_dim.22 = bf16[2048,4,128]{2,1,0:T(4,128)(2,1)S(1)} broadcast(bf16[2048,4]{1,0:T(8,128)(2,1)S(1)} %bitcast.47), dimensions={0,1} | broadcast | bytes 2113536 | tf_op jit(solution)/shard_map/broadcast_in_dim | solution.py:36
  198.8 9.3 %fusion.5 = bf16[16,128,512]{2,1,0:T(8,128)(2,1)} fusion(bf16[2048,512]{1,0:T(8,128)(2,1)S(1)} %copy-done.2, bf16[256,8,4,128]{3,2,1,0:T(4,128)(2,1)S(1)} %bitcast.46, bf16[16,128,1,2048]{3,1,0,2:T(8,128)(2,1)} %all-gather.6.cloned.1.call-done), kind=kOutput, calls=%fused_computation.7 | convolution fusion | flops 4297064448 | bytes 14680064 | tf_op jit(solution)/shard_map/dot_general | solution.py:44
  (15 shorter events, 0.1 us)
Async XLA Ops:
  7.4 58.8 %copy-start = (bf16[16,1,4,32,128]{4,3,2,1,0:T(8,128)(2,1)S(1)}, bf16[16,1,4,32,128]{4,3,2,1,0:T(8,128)(2,1)}, u32[]{:S(2)}) copy-start(bf16[16,1,4,32,128]{4,3,2,1,0:T(8,128)(2,1)} %param.7) | copy-start | bytes 1572868
  7.4 113.9 %reduce-scatter.2.cloned.1.call-start = ((), (), s32[]{:S(2)}) async-start(), calls=%async_computation.2 | async-start | bytes 5242880 | tf_op jit(solution)/shard_map/reduce_scatter | solution.py:31
  68.9 54.5 %copy-start.1 = (s32[16,4]{0,1:T(4,128)S(1)}, s32[16,4]{0,1:T(4,128)}, u32[]{:S(2)}) copy-start(s32[16,4]{0,1:T(4,128)} %param.13) | copy-start | bytes 772
  68.9 54.6 %all-gather.4.cloned.1.call-start = ((), (), s32[]{:S(2)}) async-start(), calls=%async_computation.3 | async-start | bytes 2359296 | tf_op jit(solution)/shard_map/all_gather | solution.py:35
  69.5 123.4 %all-gather.6.cloned.1.call-start = ((), (), s32[]{:S(2)}) async-start(), calls=%async_computation.4 | async-start | bytes 8912896 | tf_op jit(solution)/shard_map/all_gather | solution.py:41
  123.5 75.3 %copy-start.2 = (bf16[2048,512]{1,0:T(8,128)(2,1)S(1)}, bf16[2048,512]{1,0:T(8,128)(2,1)}, u32[]{:S(2)}) copy-start(bf16[2048,512]{1,0:T(8,128)(2,1)} %all-gather.4.cloned.1.call-done) | copy-start | bytes 6291460
Sparse Core Ops, SparseCore 0:
  69.0 52.1 reduce-scatter.1
Sparse Core Ops, SparseCore 1:
  71.5 40.2 all-gather.3
  123.5 69.4 all-gather.5
where the time goes:
time: 216 us
  waiting for transfers between devices  122 us (56%)
  blocking collectives  53.5 us (25%)
  between operations  16.3 us (8%)
  matrix products  12 us (6%)
  local copies, waits for them, and re-layouts  8.79 us (4%)
  other arithmetic  3.2 us (1%)
    all_gather x1, waiting for transfers between devices, local(): piece = lax.all_gather(half_local, 'ao', axis=2, tiled=True)  69.4 us
    reduce_scatter x1, waiting for transfers between devices, local(): lax.psum_scatter(partial_term, 'orb', scatter_dimension=1, tiled=True)  51.7 us
    unnamed x1, blocking collectives  29.8 us
    all_gather x1, blocking collectives, local(): lax.all_gather(occupied_coeff, 'ao', axis=0, tiled=True)  16.4 us
    dot_general x1, matrix products, local(): product = jnp.dot(flat, vir_masked, preferred_element_type=jnp.float32)  9.32 us
    all_to_all x1, blocking collectives, local(): lax.all_to_all(picked, 'orb', split_axis=2, concat_axis=3, tiled=True)  7.31 us
    broadcast_in_dim x1, local copies, waits for them, and re-layouts, local(): jnp.repeat(jnp.repeat(virtual_domain, block_size, axis=0), block_size, ax...  5.78 us
  transfers between devices with their start and end apart: 3, of which 2 were waited for; matrix products, arithmetic and copies ran while one was open for 1% of the time, Pallas kernels for 0%

commit v1 on v0

--- a/solution.py
+++ b/solution.py
@@ -2,6 +2,19 @@
 import jax.numpy as jnp
 from jax import lax
 from jax.sharding import PartitionSpec as P
+
+
+def ring_gather(x, axis, dim):
+    ways = lax.axis_size(axis)
+    up = [(d, (d + 1) % ways) for d in range(ways)]
+    down = [(d, (d - 1) % ways) for d in range(ways)]
+    earlier, later = ([x], [x])
+    for _ in range(ways // 2):
+        earlier.append(lax.ppermute(earlier[-1], axis, up))
+    for _ in range((ways - 1) // 2):
+        later.append(lax.ppermute(later[-1], axis, down))
+    line = jnp.concatenate([*earlier[::-1], *later[1:]], axis=dim)
+    return jnp.roll(line, (lax.axis_index(axis) - ways // 2) * x.shape[dim], axis=dim)
 
 
 def local(
@@ -38,7 +51,7 @@
     ).astype(jnp.bfloat16)
     vir_masked = vir_rows * vir_mask
     vir_width = vir_masked.shape[1]
-    piece = lax.all_gather(half_local, "ao", axis=2, tiled=True)
+    piece = ring_gather(half_local, "ao", 2)
     count = piece.shape[2]
     flat = piece.reshape(slab_rows * occ_width, count)
     product = jnp.dot(flat, vir_masked, preferred_element_type=jnp.float32)

time: 216 us -> 271 us (1.25)
  the two profiles are of different devices: /device:TPU:1 before, /device:TPU:32 now
where the time goes in v1:
time: 271 us; the launch traced here: 270 us
  waiting for transfers between devices  110 us (41%)
  local copies, waits for them, and re-layouts  53.2 us (20%)
  blocking collectives  49.6 us (18%)
  starting transfers between devices  21.5 us (8%)
  between operations  16.4 us (6%)
  matrix products  12.5 us (5%)
  other arithmetic  6.29 us (2%)
    reduce_scatter x1, waiting for transfers between devices, local(): lax.psum_scatter(partial_term, 'orb', scatter_dimension=1, tiled=True)  55.1 us
    ppermute x8, waiting for transfers between devices, ring_gather(): earlier.append(lax.ppermute(earlier[-1], axis, up))  51.2 us
    unnamed x64, local copies, waits for them, and re-layouts  45.5 us
    unnamed x1, blocking collectives  23.6 us
    ppermute x7, starting transfers between devices, ring_gather(): later.append(lax.ppermute(later[-1], axis, down))  21.4 us
    all_gather x1, blocking collectives, local(): lax.all_gather(occupied_coeff, 'ao', axis=0, tiled=True)  16.6 us
    dot_general x1, matrix products, local(): product = jnp.dot(flat, vir_masked, preferred_element_type=jnp.float32)  9.84 us
    all_to_all x1, blocking collectives, local(): lax.all_to_all(picked, 'orb', split_axis=2, concat_axis=3, tiled=True)  9.44 us
  transfers between devices with their start and end apart: 17, of which 13 were waited for; matrix products, arithmetic and copies ran while one was open for 17% of the time, Pallas kernels for 0%

profile of v1, /device:TPU:32, one launch (start us, length us, event | category | flops | bytes accessed | tf_op | source)
XLA Modules:
  0.0 269.5 jit_solution(3315399587837178091)
XLA Ops:
  10.2 23.6 %all-reduce = bf16[16]{0:T(256)(128)(2,1)S(1)} all-reduce(bf16[16]{0:T(256)(128)(2,1)S(1)} %dynamic-update-slice), channel_id=1, replica_groups=mesh['aux'=8,'ao'=16,'orb'=4] {'ao'}, use_global_device_ids=true, to_apply=%add | all-reduce | flops 16 | bytes 64
  33.9 16.6 %all_gather.11 = bf16[2048,128]{1,0:T(8,128)(2,1)S(1)} all-gather(bf16[128,128]{1,0:T(8,128)(2,1)} %param.10), channel_id=1, replica_groups=mesh['aux'=8,'ao'=16,'orb'=4] {'ao'}, dimensions={0}, use_global_device_ids=true | all-gather | bytes 557056 | tf_op jit(solution)/shard_map/all_gather | solution.py:30
  52.9 9.4 %all_to_all.15 = bf16[1,4,128,128]{3,1,0,2:T(4,128)(2,1)S(1)} all-to-all(bf16[1,4,128,128]{3,1,0,2:T(4,128)(2,1)S(1)} %copy.14), channel_id=1, replica_groups=mesh['aux'=8,'ao'=16,'orb'=4] {'orb'}, dimensions={2} | all-to-all | bytes 262144 | tf_op jit(solution)/shard_map/all_to_all | solution.py:40
  62.5 2.7 %convolution_bitcast_fusion = f32[16,512,1,128]{3,1,0,2:T(8,128)} fusion(bf16[4,32,512,1]{2,1,0,3:T(8,128)(2,1)S(1)} %reshape.69, bf16[16,1,4,32,128]{4,3,2,1,0:T(8,128)(2,1)S(1)} %copy-done), kind=kOutput, calls=%fused_computation.3 | convolution fusion | flops 268435456 | bytes 4849664 | tf_op jit(solution)/shard_map/nkri,pnkrv->pinv/dot_general | solution.py:41
  65.3 55.1 %reduce-scatter.2.cloned.1.call-done = f32[16,128,1,128]{3,1,0,2:T(8,128)} async-done(((f32[16,512,1,128]{3,1,0,2:T(8,128)}), f32[16,128,1,128]{3,1,0,2:T(8,128)}) %reduce-scatter.2.cloned.1.call-update) | async-done | bytes 1048592 | tf_op jit(solution)/shard_map/reduce_scatter | solution.py:44
  121.8 9.8 %collective-permute-done = bf16[16,128,128]{2,1,0:T(8,128)(2,1)S(1)} collective-permute-done((bf16[16,128,128]{2,1,0:T(8,128)(2,1)S(1)}, bf16[16,128,128]{2,1,0:T(8,128)(2,1)S(1)}, u32[]{:S(2)}, u32[]{:S(2)}) %collective-permute-start) | collective-permute-done | bytes 524320 | tf_op jit(solution)/shard_map/ppermute | solution.py:13
  131.6 3.0 %collective-permute-start.8 = (bf16[16,128,128]{2,1,0:T(8,128)(2,1)S(1)}, bf16[16,128,128]{2,1,0:T(8,128)(2,1)S(1)}, u32[]{:S(2)}, u32[]{:S(2)}) collective-permute-start(bf16[16,128,128]{2,1,0:T(8,128)(2,1)S(1)} %convert_bitcast_fusion), channel_id=1, source_target_pairs={{0,60},{4,0},{8,4},{12,8},{16,12},{20,16},{24,20},{28,24},{32,28},... | collective-permute-start | bytes 1572872 | tf_op jit(solution)/shard_map/ppermute | solution.py:15
  134.6 6.9 %collective-permute-done.1 = bf16[16,128,128]{2,1,0:T(8,128)(2,1)S(1)} collective-permute-done((bf16[16,128,128]{2,1,0:T(8,128)(2,1)S(1)}, bf16[16,128,128]{2,1,0:T(8,128)(2,1)S(1)}, u32[]{:S(2)}, u32[]{:S(2)}) %collective-permute-start.1) | collective-permute-done | bytes 524320 | tf_op jit(solution)/shard_map/ppermute | solution.py:13
  141.4 3.0 %collective-permute-start.9 = (bf16[16,128,128]{2,1,0:T(8,128)(2,1)S(1)}, bf16[16,128,128]{2,1,0:T(8,128)(2,1)S(1)}, u32[]{:S(2)}, u32[]{:S(2)}) collective-permute-start(bf16[16,128,128]{2,1,0:T(8,128)(2,1)S(1)} %collective-permute-done.8), channel_id=1, source_target_pairs={{0,60},{4,0},{8,4},{12,8},{16,12},{20,16},{24,20},{28,24},{32,28},... | collective-permute-start | bytes 1572872 | tf_op jit(solution)/shard_map/ppermute | solution.py:15
  144.4 6.9 %collective-permute-done.2 = bf16[16,128,128]{2,1,0:T(8,128)(2,1)S(1)} collective-permute-done((bf16[16,128,128]{2,1,0:T(8,128)(2,1)S(1)}, bf16[16,128,128]{2,1,0:T(8,128)(2,1)S(1)}, u32[]{:S(2)}, u32[]{:S(2)}) %collective-permute-start.2) | collective-permute-done | bytes 524320 | tf_op jit(solution)/shard_map/ppermute | solution.py:13
  152.1 2.9 %collective-permute-start.10 = (bf16[16,128,128]{2,1,0:T(8,128)(2,1)S(1)}, bf16[16,128,128]{2,1,0:T(8,128)(2,1)S(1)}, u32[]{:S(2)}, u32[]{:S(2)}) collective-permute-start(bf16[16,128,128]{2,1,0:T(8,128)(2,1)S(1)} %collective-permute-done.9), channel_id=1, source_target_pairs={{0,60},{4,0},{8,4},{12,8},{16,12},{20,16},{24,20},{28,24},{32,28},... | collective-permute-start | bytes 1572872 | tf_op jit(solution)/shard_map/ppermute | solution.py:15
  155.0 6.0 %collective-permute-done.3 = bf16[16,128,128]{2,1,0:T(8,128)(2,1)S(1)} collective-permute-done((bf16[16,128,128]{2,1,0:T(8,128)(2,1)S(1)}, bf16[16,128,128]{2,1,0:T(8,128)(2,1)S(1)}, u32[]{:S(2)}, u32[]{:S(2)}) %collective-permute-start.3) | collective-permute-done | bytes 524320 | tf_op jit(solution)/shard_map/ppermute | solution.py:13
  161.7 3.1 %collective-permute-start.11 = (bf16[16,128,128]{2,1,0:T(8,128)(2,1)S(1)}, bf16[16,128,128]{2,1,0:T(8,128)(2,1)S(1)}, u32[]{:S(2)}, u32[]{:S(2)}) collective-permute-start(bf16[16,128,128]{2,1,0:T(8,128)(2,1)S(1)} %collective-permute-done.10), channel_id=1, source_target_pairs={{0,60},{4,0},{8,4},{12,8},{16,12},{20,16},{24,20},{28,24},{32,28},... | collective-permute-start | bytes 1572872 | tf_op jit(solution)/shard_map/ppermute | solution.py:15
  164.9 6.0 %collective-permute-done.4 = bf16[16,128,128]{2,1,0:T(8,128)(2,1)S(1)} collective-permute-done((bf16[16,128,128]{2,1,0:T(8,128)(2,1)S(1)}, bf16[16,128,128]{2,1,0:T(8,128)(2,1)S(1)}, u32[]{:S(2)}, u32[]{:S(2)}) %collective-permute-start.4) | collective-permute-done | bytes 524320 | tf_op jit(solution)/shard_map/ppermute | solution.py:13
  172.4 3.1 %collective-permute-start.12 = (bf16[16,128,128]{2,1,0:T(8,128)(2,1)S(1)}, bf16[16,128,128]{2,1,0:T(8,128)(2,1)}, u32[]{:S(2)}, u32[]{:S(2)}) collective-permute-start(bf16[16,128,128]{2,1,0:T(8,128)(2,1)S(1)} %collective-permute-done.11), channel_id=1, source_target_pairs={{0,60},{4,0},{8,4},{12,8},{16,12},{20,16},{24,20},{28,24},{32,28},... | collective-permute-start | bytes 1572872 | tf_op jit(solution)/shard_map/ppermute | solution.py:15
  175.5 5.2 %collective-permute-done.5 = bf16[16,128,128]{2,1,0:T(8,128)(2,1)S(1)} collective-permute-done((bf16[16,128,128]{2,1,0:T(8,128)(2,1)S(1)}, bf16[16,128,128]{2,1,0:T(8,128)(2,1)S(1)}, u32[]{:S(2)}, u32[]{:S(2)}) %collective-permute-start.5) | collective-permute-done | bytes 524320 | tf_op jit(solution)/shard_map/ppermute | solution.py:13
  182.2 3.2 %collective-permute-start.13 = (bf16[16,128,128]{2,1,0:T(8,128)(2,1)}, bf16[16,128,128]{2,1,0:T(8,128)(2,1)}, u32[]{:S(2)}, u32[]{:S(2)}) collective-permute-start(bf16[16,128,128]{2,1,0:T(8,128)(2,1)} %collective-permute-done.12), channel_id=1, source_target_pairs={{0,60},{4,0},{8,4},{12,8},{16,12},{20,16},{24,20},{28,24},{32,28},... | collective-permute-start | bytes 1572872 | tf_op jit(solution)/shard_map/ppermute | solution.py:15
  185.4 5.2 %collective-permute-done.6 = bf16[16,128,128]{2,1,0:T(8,128)(2,1)} collective-permute-done((bf16[16,128,128]{2,1,0:T(8,128)(2,1)S(1)}, bf16[16,128,128]{2,1,0:T(8,128)(2,1)}, u32[]{:S(2)}, u32[]{:S(2)}) %collective-permute-start.6) | collective-permute-done | bytes 524320 | tf_op jit(solution)/shard_map/ppermute | solution.py:13
  192.4 3.1 %collective-permute-start.14 = (bf16[16,128,128]{2,1,0:T(8,128)(2,1)}, bf16[16,128,128]{2,1,0:T(8,128)(2,1)S(1)}, u32[]{:S(2)}, u32[]{:S(2)}) collective-permute-start(bf16[16,128,128]{2,1,0:T(8,128)(2,1)} %collective-permute-done.13), channel_id=1, source_target_pairs={{0,60},{4,0},{8,4},{12,8},{16,12},{20,16},{24,20},{28,24},{32,28},... | collective-permute-start | bytes 1572872 | tf_op jit(solution)/shard_map/ppermute | solution.py:15
  195.5 5.2 %collective-permute-done.7 = bf16[16,128,128]{2,1,0:T(8,128)(2,1)} collective-permute-done((bf16[16,128,128]{2,1,0:T(8,128)(2,1)}, bf16[16,128,128]{2,1,0:T(8,128)(2,1)}, u32[]{:S(2)}, u32[]{:S(2)}) %collective-permute-start.7) | collective-permute-done | bytes 524320 | tf_op jit(solution)/shard_map/ppermute | solution.py:13
  214.1 2.2 constant_dynamic-update-slice_fusion.23
  241.6 2.0 constant_dynamic-update-slice_fusion.2
  246.5 5.8 %broadcast_in_dim.22 = bf16[2048,4,128]{2,1,0:T(4,128)(2,1)S(1)} broadcast(bf16[2048,4]{1,0:T(8,128)(2,1)S(1)} %bitcast.48), dimensions={0,1} | broadcast | bytes 2113536 | tf_op jit(solution)/shard_map/broadcast_in_dim | solution.py:49
  252.3 9.8 %fusion.5 = bf16[16,128,512]{2,1,0:T(8,128)(2,1)} fusion(bf16[2048,512]{1,0:T(8,128)(2,1)} %all-gather.2.cloned.1.call-done, bf16[256,8,4,128]{3,2,1,0:T(4,128)(2,1)S(1)} %bitcast.47, bf16[16,128,4096]{2,1,0:T(8,128)(2,1)} %constant_dynamic-update-slice_fusion, s32[]{:T(128)S(6)} %select_n.18), kind=kOutput, calls=%fused_computation.7 | convolution fusion | flops 4297064448 | bytes 14680068 | tf_op jit(solution)/shard_map/dot_general | solution.py:57
  (100 shorter events, 53.4 us)
Async XLA Ops:
  7.4 55.2 %copy-start = (bf16[16,1,4,32,128]{4,3,2,1,0:T(8,128)(2,1)S(1)}, bf16[16,1,4,32,128]{4,3,2,1,0:T(8,128)(2,1)}, u32[]{:S(2)}) copy-start(bf16[16,1,4,32,128]{4,3,2,1,0:T(8,128)(2,1)} %param.7) | copy-start | bytes 1572868
  7.4 113.0 %reduce-scatter.2.cloned.1.call-start = ((), (), s32[]{:S(2)}) async-start(), calls=%async_computation.2 | async-start | bytes 5242880 | tf_op jit(solution)/shard_map/reduce_scatter | solution.py:44
  65.3 181.1 %all-gather.2.cloned.1.call-start = ((), (), s32[]{:S(2)}) async-start(), calls=%async_computation.3 | async-start | bytes 2359296 | tf_op jit(solution)/shard_map/all_gather | solution.py:48
  120.4 116.6 %copy-start.1 = (f32[16,128,1,128]{3,1,0,2:T(8,128)S(1)}, f32[16,128,1,128]{3,1,0,2:T(8,128)}, u32[]{:S(2)}) copy-start(f32[16,128,1,128]{3,1,0,2:T(8,128)} %reduce-scatter.2.cloned.1.call-done) | copy-start | bytes 3145732
  121.8 9.8 %collective-permute-start = (bf16[16,128,128]{2,1,0:T(8,128)(2,1)S(1)}, bf16[16,128,128]{2,1,0:T(8,128)(2,1)S(1)}, u32[]{:S(2)}, u32[]{:S(2)}) collective-permute-start(bf16[16,128,128]{2,1,0:T(8,128)(2,1)S(1)} %convert_bitcast_fusion), channel_id=1, source_target_pairs={{0,4},{4,8},{8,12},{12,16},{16,20},{20,24},{24,28},{28,32},{32,36}... | collective-permute-start | bytes 1572872 | tf_op jit(solution)/shard_map/ppermute | solution.py:13
  131.6 9.8 %collective-permute-start.1 = (bf16[16,128,128]{2,1,0:T(8,128)(2,1)S(1)}, bf16[16,128,128]{2,1,0:T(8,128)(2,1)S(1)}, u32[]{:S(2)}, u32[]{:S(2)}) collective-permute-start(bf16[16,128,128]{2,1,0:T(8,128)(2,1)S(1)} %collective-permute-done), channel_id=1, source_target_pairs={{0,4},{4,8},{8,12},{12,16},{16,20},{20,24},{24,28},{28,32},{32,36}... | collective-permute-start | bytes 1572872 | tf_op jit(solution)/shard_map/ppermute | solution.py:13
  131.6 9.8 %collective-permute-start.8 = (bf16[16,128,128]{2,1,0:T(8,128)(2,1)S(1)}, bf16[16,128,128]{2,1,0:T(8,128)(2,1)S(1)}, u32[]{:S(2)}, u32[]{:S(2)}) collective-permute-start(bf16[16,128,128]{2,1,0:T(8,128)(2,1)S(1)} %convert_bitcast_fusion), channel_id=1, source_target_pairs={{0,60},{4,0},{8,4},{12,8},{16,12},{20,16},{24,20},{28,24},{32,28},... | collective-permute-start | bytes 1572872 | tf_op jit(solution)/shard_map/ppermute | solution.py:15
  141.4 9.8 %collective-permute-start.2 = (bf16[16,128,128]{2,1,0:T(8,128)(2,1)S(1)}, bf16[16,128,128]{2,1,0:T(8,128)(2,1)S(1)}, u32[]{:S(2)}, u32[]{:S(2)}) collective-permute-start(bf16[16,128,128]{2,1,0:T(8,128)(2,1)S(1)} %collective-permute-done.1), channel_id=1, source_target_pairs={{0,4},{4,8},{8,12},{12,16},{16,20},{20,24},{24,28},{28,32},{32,36}... | collective-permute-start | bytes 1572872 | tf_op jit(solution)/shard_map/ppermute | solution.py:13
  141.4 9.8 %collective-permute-start.9 = (bf16[16,128,128]{2,1,0:T(8,128)(2,1)S(1)}, bf16[16,128,128]{2,1,0:T(8,128)(2,1)S(1)}, u32[]{:S(2)}, u32[]{:S(2)}) collective-permute-start(bf16[16,128,128]{2,1,0:T(8,128)(2,1)S(1)} %collective-permute-done.8), channel_id=1, source_target_pairs={{0,60},{4,0},{8,4},{12,8},{16,12},{20,16},{24,20},{28,24},{32,28},... | collective-permute-start | bytes 1572872 | tf_op jit(solution)/shard_map/ppermute | solution.py:15
  151.2 9.8 %collective-permute-start.3 = (bf16[16,128,128]{2,1,0:T(8,128)(2,1)S(1)}, bf16[16,128,128]{2,1,0:T(8,128)(2,1)S(1)}, u32[]{:S(2)}, u32[]{:S(2)}) collective-permute-start(bf16[16,128,128]{2,1,0:T(8,128)(2,1)S(1)} %collective-permute-done.2), channel_id=1, source_target_pairs={{0,4},{4,8},{8,12},{12,16},{16,20},{20,24},{24,28},{28,32},{32,36}... | collective-permute-start | bytes 1572872 | tf_op jit(solution)/shard_map/ppermute | solution.py:13
  152.1 9.6 %collective-permute-start.10 = (bf16[16,128,128]{2,1,0:T(8,128)(2,1)S(1)}, bf16[16,128,128]{2,1,0:T(8,128)(2,1)S(1)}, u32[]{:S(2)}, u32[]{:S(2)}) collective-permute-start(bf16[16,128,128]{2,1,0:T(8,128)(2,1)S(1)} %collective-permute-done.9), channel_id=1, source_target_pairs={{0,60},{4,0},{8,4},{12,8},{16,12},{20,16},{24,20},{28,24},{32,28},... | collective-permute-start | bytes 1572872 | tf_op jit(solution)/shard_map/ppermute | solution.py:15
  161.1 9.8 %collective-permute-start.4 = (bf16[16,128,128]{2,1,0:T(8,128)(2,1)S(1)}, bf16[16,128,128]{2,1,0:T(8,128)(2,1)S(1)}, u32[]{:S(2)}, u32[]{:S(2)}) collective-permute-start(bf16[16,128,128]{2,1,0:T(8,128)(2,1)S(1)} %collective-permute-done.3), channel_id=1, source_target_pairs={{0,4},{4,8},{8,12},{12,16},{16,20},{20,24},{24,28},{28,32},{32,36}... | collective-permute-start | bytes 1572872 | tf_op jit(solution)/shard_map/ppermute | solution.py:13
  161.7 9.8 %collective-permute-start.11 = (bf16[16,128,128]{2,1,0:T(8,128)(2,1)S(1)}, bf16[16,128,128]{2,1,0:T(8,128)(2,1)S(1)}, u32[]{:S(2)}, u32[]{:S(2)}) collective-permute-start(bf16[16,128,128]{2,1,0:T(8,128)(2,1)S(1)} %collective-permute-done.10), channel_id=1, source_target_pairs={{0,60},{4,0},{8,4},{12,8},{16,12},{20,16},{24,20},{28,24},{32,28},... | collective-permute-start | bytes 1572872 | tf_op jit(solution)/shard_map/ppermute | solution.py:15
  170.9 9.8 %collective-permute-start.5 = (bf16[16,128,128]{2,1,0:T(8,128)(2,1)S(1)}, bf16[16,128,128]{2,1,0:T(8,128)(2,1)S(1)}, u32[]{:S(2)}, u32[]{:S(2)}) collective-permute-start(bf16[16,128,128]{2,1,0:T(8,128)(2,1)S(1)} %collective-permute-done.4), channel_id=1, source_target_pairs={{0,4},{4,8},{8,12},{12,16},{16,20},{20,24},{24,28},{28,32},{32,36}... | collective-permute-start | bytes 1572872 | tf_op jit(solution)/shard_map/ppermute | solution.py:13
  172.4 9.8 %collective-permute-start.12 = (bf16[16,128,128]{2,1,0:T(8,128)(2,1)S(1)}, bf16[16,128,128]{2,1,0:T(8,128)(2,1)}, u32[]{:S(2)}, u32[]{:S(2)}) collective-permute-start(bf16[16,128,128]{2,1,0:T(8,128)(2,1)S(1)} %collective-permute-done.11), channel_id=1, source_target_pairs={{0,60},{4,0},{8,4},{12,8},{16,12},{20,16},{24,20},{28,24},{32,28},... | collective-permute-start | bytes 1572872 | tf_op jit(solution)/shard_map/ppermute | solution.py:15
  180.7 9.9 %collective-permute-start.6 = (bf16[16,128,128]{2,1,0:T(8,128)(2,1)S(1)}, bf16[16,128,128]{2,1,0:T(8,128)(2,1)}, u32[]{:S(2)}, u32[]{:S(2)}) collective-permute-start(bf16[16,128,128]{2,1,0:T(8,128)(2,1)S(1)} %collective-permute-done.5), channel_id=1, source_target_pairs={{0,4},{4,8},{8,12},{12,16},{16,20},{20,24},{24,28},{28,32},{32,36}... | collective-permute-start | bytes 1572872 | tf_op jit(solution)/shard_map/ppermute | solution.py:13
  182.2 10.2 %collective-permute-start.13 = (bf16[16,128,128]{2,1,0:T(8,128)(2,1)}, bf16[16,128,128]{2,1,0:T(8,128)(2,1)}, u32[]{:S(2)}, u32[]{:S(2)}) collective-permute-start(bf16[16,128,128]{2,1,0:T(8,128)(2,1)} %collective-permute-done.12), channel_id=1, source_target_pairs={{0,60},{4,0},{8,4},{12,8},{16,12},{20,16},{24,20},{28,24},{32,28},... | collective-permute-start | bytes 1572872 | tf_op jit(solution)/shard_map/ppermute | solution.py:15
  190.6 10.1 %collective-permute-start.7 = (bf16[16,128,128]{2,1,0:T(8,128)(2,1)}, bf16[16,128,128]{2,1,0:T(8,128)(2,1)}, u32[]{:S(2)}, u32[]{:S(2)}) collective-permute-start(bf16[16,128,128]{2,1,0:T(8,128)(2,1)} %collective-permute-done.6), channel_id=1, source_target_pairs={{0,4},{4,8},{8,12},{12,16},{16,20},{20,24},{24,28},{28,32},{32,36}... | collective-permute-start | bytes 1572872 | tf_op jit(solution)/shard_map/ppermute | solution.py:13
  191.5 41.9 %copy-start.11 = (bf16[16,128,128]{2,1,0:T(8,128)(2,1)S(1)}, bf16[16,128,128]{2,1,0:T(8,128)(2,1)}, u32[]{:S(2)}) copy-start(bf16[16,128,128]{2,1,0:T(8,128)(2,1)} %copy-done.10) | copy-start | bytes 1572868
  191.5 42.8 %copy-start.5 = (bf16[16,128,128]{2,1,0:T(8,128)(2,1)S(1)}, bf16[16,128,128]{2,1,0:T(8,128)(2,1)}, u32[]{:S(2)}) copy-start(bf16[16,128,128]{2,1,0:T(8,128)(2,1)} %copy-done.4) | copy-start | bytes 1572868
  191.5 47.5 %copy-start.3 = (bf16[16,128,128]{2,1,0:T(8,128)(2,1)S(1)}, bf16[16,128,128]{2,1,0:T(8,128)(2,1)}, u32[]{:S(2)}) copy-start(bf16[16,128,128]{2,1,0:T(8,128)(2,1)} %copy-done.2) | copy-start | bytes 1572868
  191.5 48.3 %copy-start.7 = (bf16[16,128,128]{2,1,0:T(8,128)(2,1)S(1)}, bf16[16,128,128]{2,1,0:T(8,128)(2,1)}, u32[]{:S(2)}) copy-start(bf16[16,128,128]{2,1,0:T(8,128)(2,1)} %copy-done.6) | copy-start | bytes 1572868
  191.5 49.2 %copy-start.9 = (bf16[16,128,128]{2,1,0:T(8,128)(2,1)S(1)}, bf16[16,128,128]{2,1,0:T(8,128)(2,1)}, u32[]{:S(2)}) copy-start(bf16[16,128,128]{2,1,0:T(8,128)(2,1)} %copy-done.8) | copy-start | bytes 1572868
  192.4 34.4 %collective-permute-start.14 = (bf16[16,128,128]{2,1,0:T(8,128)(2,1)}, bf16[16,128,128]{2,1,0:T(8,128)(2,1)S(1)}, u32[]{:S(2)}, u32[]{:S(2)}) collective-permute-start(bf16[16,128,128]{2,1,0:T(8,128)(2,1)} %collective-permute-done.13), channel_id=1, source_target_pairs={{0,60},{4,0},{8,4},{12,8},{16,12},{20,16},{24,20},{28,24},{32,28},... | collective-permute-start | bytes 1572872 | tf_op jit(solution)/shard_map/ppermute | solution.py:15
  (9 other events, 142.0 us)
Sparse Core Ops, SparseCore 0:
  65.4 54.9 reduce-scatter.1
Sparse Core Ops, SparseCore 1:
  190.7 44.4 all-gather.1
